TPU v7x, 256 devices: a whole 4x4x8 slice. The times are simulated.
256 devices in a mesh: ens: 16 (over z, y_hi), mp: 16 (over x, y_lo, core).
Axes of the slice: x: 4, y: 4 (y_hi: 2, y_lo: 2; y = y_hi * 2 + y_lo), z: 8, core: 2. Of those that a mesh axis runs over, the one named last changes fastest.
Arguments:
- tokens: bfloat16 [16, 8192, 1024], P('ens', 'mp'), may hold values from -6 to 6
- ln_gain: float32 [1024], replicated, may hold values from 0.5 to 1.5
- w_qkv: bfloat16 [1024, 3072], replicated, may hold values from -1 to 1
- w_out: bfloat16 [1024, 1024], replicated, may hold values from -0.75 to 0.75
- neighbours: int32 [4, 32768], P(None, 'mp'), may hold values from 0 to 8191, as said below
- edge_weights: float32 [4, 32768], P(None, 'mp'), may hold values from 0.2 to 1
- w_dec: bfloat16 [100, 1024], replicated, may hold values from -0.1875 to 0.1875
- truth: float32 [100, 32768], P(None, ('mp', 'ens')), may hold values from -6 to 6
Outputs:
- crps_score: float32 [100, 32768], P(None, ('mp', 'ens'))
Inputs may be any that keep to these rules, and one draw needn't show every extreme that they name: `neighbours`: the tokens of point g are among tokens g // 2048 * 512 to g // 2048 * 512 + 511 of its member.
All inputs are finite; a program needn't handle non-finite values.
Results may differ from a plain program's by a relative error of at most 0.0028.
The roundings to bfloat16 on the way count: a program that leaves them out, or rounds other values in their place, can miss the bound.
Values may be sent and summed in bfloat16 or wider, within the bound.
A program may use at most 128 MiB of HBM per device.

v0:
```python
import jax
import jax.numpy as jnp
from jax import lax
from jax.sharding import PartitionSpec as P

HEADS = 16
NEIGH = 4
HALF = 512
ALPHA = 0.95


def layer_norm(inputs, ln_gain):
    values = inputs.astype(jnp.float32)
    average = jnp.mean(values, axis=-1, keepdims=True)
    centred = values - average
    variance = jnp.mean(centred * centred, axis=-1, keepdims=True)
    return (centred * lax.rsqrt(variance + 1e-05) * ln_gain).astype(jnp.bfloat16)


def attend(queries, key_rows, value_rows, first_row, seq_tokens):
    count = queries.shape[1]
    head_dim = queries.shape[-1]
    scores = jnp.einsum(
        "mqhe,mkhe->mhqk", queries, key_rows, preferred_element_type=jnp.float32
    ) / jnp.sqrt(jnp.float32(head_dim))
    query_pos = first_row + jnp.arange(count, dtype=jnp.int32)
    key_pos = first_row - HALF + jnp.arange(count + 2 * HALF, dtype=jnp.int32)
    allowed = (
        (key_pos[None, :] >= 0)
        & (key_pos[None, :] < seq_tokens)
        & (jnp.abs(key_pos[None, :] - query_pos[:, None]) <= HALF)
    )
    scores = jnp.where(allowed[None, None], scores, -1e30)
    top = jnp.max(scores, axis=-1, keepdims=True)
    expo = jnp.exp(scores - top)
    weights = (expo / jnp.sum(expo, axis=-1, keepdims=True)).astype(jnp.bfloat16)
    context = jnp.einsum("mhqk,mkhe->mqhe", weights, value_rows, preferred_element_type=jnp.float32)
    return context.astype(jnp.bfloat16)


def shards(tokens, ln_gain, w_qkv, w_out, neighbours, edge_weights, w_dec, truth):
    members_here, tok_rows, model_width = tokens.shape
    lane_count = lax.axis_size("mp")
    lane_index = lax.axis_index("mp")
    seq_tokens = tok_rows * lane_count
    head_count = HEADS
    head_dim = model_width // head_count
    normed = layer_norm(tokens, ln_gain)
    projected = jnp.einsum("mtd,de->mte", normed, w_qkv, preferred_element_type=jnp.float32).astype(
        jnp.bfloat16
    )
    by_head = projected.reshape(members_here, tok_rows, 3, head_count, head_dim)
    regroup = lax.all_to_all(by_head, "mp", split_axis=3, concat_axis=1, tiled=True)
    local_heads = head_count // lane_count
    queries = regroup[:, :, 0]
    key_pad = jnp.pad(regroup[:, :, 1], ((0, 0), (HALF, HALF), (0, 0), (0, 0)))
    value_pad = jnp.pad(regroup[:, :, 2], ((0, 0), (HALF, HALF), (0, 0), (0, 0)))

    def block_attend(block_index):
        first_row = block_index * tok_rows
        query_block = lax.dynamic_slice_in_dim(queries, first_row, tok_rows, 1)
        key_block = lax.dynamic_slice_in_dim(key_pad, first_row, tok_rows + 2 * HALF, 1)
        value_block = lax.dynamic_slice_in_dim(value_pad, first_row, tok_rows + 2 * HALF, 1)
        return attend(query_block, key_block, value_block, first_row, seq_tokens)

    block_outs = lax.map(block_attend, jnp.arange(lane_count, dtype=jnp.int32))
    all_rows = jnp.moveaxis(block_outs, 0, 1).reshape(
        members_here, seq_tokens, local_heads, head_dim
    )
    context = lax.all_to_all(all_rows, "mp", split_axis=1, concat_axis=2, tiled=True)
    context = context.reshape(members_here, tok_rows, model_width)
    proj_out = jnp.einsum("mtd,de->mte", context, w_out, preferred_element_type=jnp.float32)
    processed = (tokens.astype(jnp.float32) + proj_out).astype(jnp.bfloat16)
    local_index = neighbours - lane_index * tok_rows
    hidden = jnp.zeros((members_here, neighbours.shape[1], model_width), jnp.float32)
    for slot_index in range(NEIGH):
        picked = jnp.take(processed, local_index[slot_index], axis=1)
        hidden = hidden + edge_weights[slot_index][None, :, None] * picked.astype(jnp.float32)
    decoded = jnp.einsum(
        "vd,mgd->mvg", w_dec, hidden.astype(jnp.bfloat16), preferred_element_type=jnp.float32
    ).astype(jnp.bfloat16)
    gathered = lax.all_to_all(decoded, "ens", split_axis=2, concat_axis=0, tiled=True).astype(
        jnp.float32
    )
    member_total = gathered.shape[0]
    skill_term = jnp.mean(jnp.abs(gathered - truth[None]), axis=0)
    spread = jnp.sum(jnp.abs(gathered[:, None] - gathered[None, :]), axis=(0, 1))
    coeff = ALPHA / (2.0 * member_total * (member_total - 1)) + (1.0 - ALPHA) / (
        2.0 * member_total * member_total
    )
    return skill_term - coeff * spread


def solution(mesh):
    in_specs = (
        P("ens", "mp", None),
        P(),
        P(),
        P(),
        P(None, "mp"),
        P(None, "mp"),
        P(),
        P(None, ("mp", "ens")),
    )
    out_specs = P(None, ("mp", "ens"))
    return jax.shard_map(shards, mesh=mesh, in_specs=in_specs, out_specs=out_specs, check_vma=False)
```

profile of v0, /device:TPU:8, one launch (start us, length us, event | category | flops | bytes accessed | tf_op | source)
XLA Modules:
  0.0 371.9 jit_solution(4626940275149164872)
XLA Ops:
  3.2 8.3 %convolution_convert_fusion = bf16[512,3072]{1,0:T(8,128)(2,1)} fusion(bf16[1024,3072]{1,0:T(8,128)(2,1)} %param.14, bf16[1,512,1024]{2,1,0:T(8,128)(2,1)} %param.12, f32[1024]{0:T(1024)} %param.13, f32[512]{0:T(512)S(1)} %add_rsqrt_fusion, f32[512]{0:T(512)S(1)} %broadcast_multiply_fusion), kind=kOutput, calls=%fused_computation.28 | convolution fusion | flops 3225419776 | bytes 10493952 | tf_op jit(solution)/shard_map/mtd,de->mte/dot_general | solution.py:49
  11.5 4.7 %copy.45 = bf16[512,3072]{0,1:T(8,128)(2,1)} copy(bf16[512,3072]{1,0:T(8,128)(2,1)} %convolution_convert_fusion) | data formatting | bytes 6291456 | tf_op jit(solution)/shard_map/convert_element_type | solution.py:49
  16.2 3.9 %copy.46 = bf16[1,512,3,16,64]{1,4,2,0,3:T(8,128)(2,1)} copy(bf16[1,512,3,16,64]{1,4,3,2,0:T(8,128)(2,1)} %bitcast.144) | data formatting | bytes 6291456 | tf_op jit(solution)/shard_map/reshape | solution.py:52
  20.2 6.5 %all-to-all-start = ((bf16[1,512,3,16,64]{1,4,2,0,3:T(8,128)(2,1)}), bf16[1,512,3,16,64]{1,4,2,0,3:T(8,128)(2,1)}, u32[]{:S(2)}, u32[]{:S(2)}) async-start(bf16[1,512,3,16,64]{1,4,2,0,3:T(8,128)(2,1)} %copy.46), calls=%async_computation | async-start | bytes 6291456 | tf_op jit(solution)/shard_map/all_to_all | solution.py:53
  26.8 42.5 %all-to-all-done = bf16[1,512,3,16,64]{1,4,2,0,3:T(8,128)(2,1)} async-done(((bf16[1,512,3,16,64]{1,4,2,0,3:T(8,128)(2,1)}), bf16[1,512,3,16,64]{1,4,2,0,3:T(8,128)(2,1)}, u32[]{:S(2)}, u32[]{:S(2)}) %all-to-all-start) | async-done | bytes 3145760 | tf_op jit(solution)/shard_map/all_to_all | solution.py:53
  74.2 92.6 %while.12 = (s32[]{:T(128)}, bf16[16,1,512,1,64]{2,4,3,1,0:T(8,128)(2,1)}, s32[16]{0:T(128)S(1)}, bf16[1,9216,1,64]{1,3,2,0:T(8,128)(2,1)S(1)}, bf16[1,8192,1,64...) while((s32[]{:T(128)}, ...), condition=%wide.region_5.6_spmd, body=%wide.region_2.5_spmd.sunk | while | flops 210803712 | bytes 9991916 | solution.py:66
  98.7 2.4 fusion.54
  150.7 2.4 fusion.54
  166.7 2.8 copy.55
  169.5 12.5 %reshape.226 = bf16[1,8192,1,64]{3,2,0,1:T(2,128)(2,1)} reshape(bf16[16,1,512,1,64]{4,2,0,3,1:T(8,128)(2,1)} %copy.55) | data formatting | bytes 2097152 | tf_op jit(solution)/shard_map/reshape;transpose | solution.py:67
  182.5 46.5 %reduce.12 = bf16[8192,64]{1,0:T(8,128)(2,1)} reduce(bf16[8192,1,1,64]{3,2,1,0:T(2,128)(2,1)} %bitcast.139, bf16[]{:T(256)} %broadcast.155), dimensions={1,2}, to_apply=%bitcast.116.reduce_sub_computation | reduce | bytes 2097154
  229.0 4.7 %reshape.227 = bf16[16,2,16384]{2,1,0:T(2,128)(2,1)} reshape(bf16[8192,64]{1,0:T(8,128)(2,1)} %reduce.12) | data formatting | bytes 2097152
  233.7 4.4 %all-to-all-start.1 = ((bf16[16,2,16384]{2,1,0:T(2,128)(2,1)}), bf16[16,2,16384]{2,1,0:T(2,128)(2,1)S(1)}, u32[]{:S(2)}, u32[]{:S(2)}) async-start(bf16[16,2,16384]{2,1,0:T(2,128)(2,1)} %reshape.227), calls=%async_computation.1 | async-start | bytes 2097152 | tf_op jit(solution)/shard_map/all_to_all | solution.py:70
  238.1 14.8 %all-to-all-done.1 = bf16[16,2,16384]{2,1,0:T(2,128)(2,1)S(1)} async-done(((bf16[16,2,16384]{2,1,0:T(2,128)(2,1)}), bf16[16,2,16384]{2,1,0:T(2,128)(2,1)S(1)}, u32[]{:S(2)}, u32[]{:S(2)}) %all-to-all-start.1) | async-done | bytes 1048608 | tf_op jit(solution)/shard_map/all_to_all | solution.py:70
  252.9 7.0 %reshape.228 = bf16[8192,1,1,64]{3,2,1,0:T(2,128)(2,1)} reshape(bf16[16,2,16384]{2,1,0:T(2,128)(2,1)S(1)} %all-to-all-done.1) | data formatting | bytes 2097152
  259.9 8.2 %copy.50 = bf16[1,8192,1,64]{1,3,2,0:T(8,128)(2,1)S(1)} copy(bf16[1,8192,1,64]{3,2,0,1:T(2,128)(2,1)} %bitcast.138) | data formatting | bytes 2097152 | tf_op jit(solution)/shard_map/all_to_all | solution.py:70
  270.6 9.6 %gather_fusion = bf16[2048,1024]{1,0:T(8,128)(2,1)} fusion(bf16[512,1024]{1,0:T(8,128)(2,1)S(1)} %fusion.31, s32[2048]{0:T(1024)S(1)} %fusion.37), kind=kCustom, calls=%fused_computation.clone | custom fusion | bytes 8396800 | tf_op jit(solution)/shard_map/jit(_take)/gather | solution.py:77
  280.3 9.7 %gather_fusion.1 = bf16[2048,1024]{1,0:T(8,128)(2,1)} fusion(bf16[512,1024]{1,0:T(8,128)(2,1)S(1)} %fusion.31, s32[2048]{0:T(1024)S(1)} %fusion.38), kind=kCustom, calls=%fused_computation.1.clone | custom fusion | bytes 8396800 | tf_op jit(solution)/shard_map/jit(_take)/gather | solution.py:77
  289.9 9.7 %gather_fusion.2 = bf16[2048,1024]{1,0:T(8,128)(2,1)} fusion(bf16[512,1024]{1,0:T(8,128)(2,1)S(1)} %fusion.31, s32[2048]{0:T(1024)S(1)} %fusion.39), kind=kCustom, calls=%fused_computation.2.clone | custom fusion | bytes 8396800 | tf_op jit(solution)/shard_map/jit(_take)/gather | solution.py:77
  299.6 9.7 %gather_fusion.3 = bf16[2048,1024]{1,0:T(8,128)(2,1)} fusion(bf16[512,1024]{1,0:T(8,128)(2,1)S(1)} %fusion.31, s32[2048]{0:T(1024)S(1)} %fusion.40), kind=kCustom, calls=%fused_computation.3.clone | custom fusion | bytes 8396800 | tf_op jit(solution)/shard_map/jit(_take)/gather | solution.py:77
  309.3 9.7 %fusion.23 = bf16[1,100,2048]{2,1,0:T(8,128)(2,1)S(1)} fusion(bf16[100,1024]{1,0:T(8,128)(2,1)S(1)} %copy-done.6, bf16[2048,1024]{1,0:T(8,128)(2,1)} %gather_fusion.3, bf16[2048,1024]{1,0:T(8,128)(2,1)} %gather_fusion.2, bf16[2048,1024]{1,0:T(8,128)(2,1)} %gather_fusion.1, bf16[2048,1024]{1,0:T(8,128)(2,1)} %gather_fusion, f32[2048]{0:T(1024)S(1)} %bitcast.160, ...), kind=kOutput, calls=%fused_computation.41 | convolution fusion | flops 453189632 | bytes 17432576 | tf_op jit(solution)/shard_map/vd,mgd->mvg/dot_general | solution.py:79
  319.7 11.8 %reduce.13 = bf16[2048,100]{1,0:T(8,128)(2,1)S(1)} reduce(bf16[2048,1,100]{2,1,0:T(2,128)(2,1)S(1)} %bitcast.147, bf16[]{:T(256)} %broadcast.155), dimensions={1}, to_apply=%bitcast.118.reduce_sub_computation | reduce | bytes 819202
  333.2 27.9 %all_to_all.42 = bf16[16,2,6400]{2,1,0:T(2,128)(2,1)S(1)} all-to-all(bf16[16,2,6400]{2,1,0:T(2,128)(2,1)S(1)} %reshape.229), channel_id=1, replica_groups=mesh['ens'=16,'mp'=16] {'ens'}, dimensions={0} | all-to-all | bytes 819200 | tf_op jit(solution)/shard_map/all_to_all | solution.py:82
  363.3 3.8 %copy.53 = bf16[1,100,2048]{2,0,1:T(2,128)(2,1)} copy(bf16[1,100,2048]{1,0,2:T(2,128)(2,1)S(1)} %bitcast.146) | data formatting | bytes 819200 | tf_op jit(solution)/shard_map/all_to_all | solution.py:82
  (155 shorter events, 96.9 us)
Async XLA Ops:
  0.0 269.0 %copy-start = (bf16[1024,1024]{1,0:T(8,128)(2,1)S(1)}, bf16[1024,1024]{1,0:T(8,128)(2,1)}, u32[]{:S(2)}) copy-start(bf16[1024,1024]{1,0:T(8,128)(2,1)} %param.15) | copy-start | bytes 6291460
  20.2 6.5 %copy-start.4 = (s32[4,2048]{1,0:T(4,128)S(1)}, s32[4,2048]{1,0:T(4,128)}, u32[]{:S(2)}) copy-start(s32[4,2048]{1,0:T(4,128)} %param.16) | copy-start | bytes 98308
  20.2 49.2 %all-to-all-start = ((bf16[1,512,3,16,64]{1,4,2,0,3:T(8,128)(2,1)}), bf16[1,512,3,16,64]{1,4,2,0,3:T(8,128)(2,1)}, u32[]{:S(2)}, u32[]{:S(2)}) async-start(bf16[1,512,3,16,64]{1,4,2,0,3:T(8,128)(2,1)} %copy.46), calls=%async_computation | async-start | bytes 6291456 | tf_op jit(solution)/shard_map/all_to_all | solution.py:53
  229.0 9.1 %copy-start.5 = (f32[4,2048]{1,0:T(4,128)S(1)}, f32[4,2048]{1,0:T(4,128)}, u32[]{:S(2)}) copy-start(f32[4,2048]{1,0:T(4,128)} %param.17) | copy-start | bytes 98308
  233.7 19.2 %all-to-all-start.1 = ((bf16[16,2,16384]{2,1,0:T(2,128)(2,1)}), bf16[16,2,16384]{2,1,0:T(2,128)(2,1)S(1)}, u32[]{:S(2)}, u32[]{:S(2)}) async-start(bf16[16,2,16384]{2,1,0:T(2,128)(2,1)} %reshape.227), calls=%async_computation.1 | async-start | bytes 2097152 | tf_op jit(solution)/shard_map/all_to_all | solution.py:70
  268.1 1.2 copy-start.2
  299.6 9.7 %copy-start.6 = (bf16[100,1024]{1,0:T(8,128)(2,1)S(1)}, bf16[100,1024]{1,0:T(8,128)(2,1)}, u32[]{:S(2)}) copy-start(bf16[100,1024]{1,0:T(8,128)(2,1)} %param.18) | copy-start | bytes 614404
  363.3 7.7 %copy-start.3 = (f32[100,128]{1,0:T(8,128)S(1)}, f32[100,128]{1,0:T(8,128)}, u32[]{:S(2)}) copy-start(f32[100,128]{1,0:T(8,128)} %param.19) | copy-start | bytes 153604
  363.3 8.6 %copy-start.1 = (bf16[1024,1024]{1,0:T(8,128)(2,1)S(1)}, bf16[1024,1024]{1,0:T(8,128)(2,1)}, u32[]{:S(2)}) copy-start(bf16[1024,1024]{1,0:T(8,128)(2,1)} %param.15) | copy-start | bytes 6291460
where the time goes:
time: 374 us; the launch traced here: 372 us
  local copies, waits for them, and re-layouts  108 us (29%)
  matrix products  80.5 us (22%)
  other arithmetic  75.6 us (20%)
  waiting for transfers between devices  57.3 us (15%)
  blocking collectives  27.9 us (7%)
  loops' own time  11.5 us (3%)
  starting transfers between devices  10.9 us (3%)
    unnamed x2, other arithmetic  58.3 us
    all_to_all x1, waiting for transfers between devices, shards(): lax.all_to_all(by_head, 'mp', split_axis=3, concat_axis=1, tiled=True)  42.5 us
    gather x4, local copies, waits for them, and re-layouts, shards(): picked = jnp.take(processed, local_index[slot_index], axis=1)  38.6 us
    dot_general x16, matrix products, attend(): jnp.einsum('mqhe,mkhe->mhqk', queries, key_rows, preferred_element_type=j...  38 us
    all_to_all x1, blocking collectives, shards(): lax.all_to_all(decoded, 'ens', split_axis=2, concat_axis=0, tiled=True)  27.9 us
    dot_general x16, matrix products, attend(): jnp.einsum('mhqk,mkhe->mqhe', weights, value_rows, preferred_element_type...  23.2 us
    unnamed x20, local copies, waits for them, and re-layouts  16.7 us
    another operation x2, local copies, waits for them, and re-layouts, shards(): jnp.moveaxis(block_outs, 0, 1)  15.3 us
  transfers between devices with their start and end apart: 2, of which 2 were waited for; matrix products, arithmetic and copies ran while one was open for 0% of the time, Pallas kernels for 0%

commit v1 on v0

--- a/solution.py
+++ b/solution.py
@@ -67,7 +67,9 @@
     all_rows = jnp.moveaxis(block_outs, 0, 1).reshape(
         members_here, seq_tokens, local_heads, head_dim
     )
-    context = lax.all_to_all(all_rows, "mp", split_axis=1, concat_axis=2, tiled=True)
+    shards_2 = jnp.split(all_rows, lax.axis_size("mp"), axis=1)
+    incoming = lax.all_to_all(jnp.stack(shards_2), "mp", 0, 0)
+    context = jnp.concatenate(incoming, axis=2)
     context = context.reshape(members_here, tok_rows, model_width)
     proj_out = jnp.einsum("mtd,de->mte", context, w_out, preferred_element_type=jnp.float32)
     processed = (tokens.astype(jnp.float32) + proj_out).astype(jnp.bfloat16)

time: 374 us -> 308 us (0.82)
  other arithmetic: 75.6 us -> 29.6 us
  local copies, waits for them, and re-layouts: 108 us -> 86.5 us
    unnamed x2 -> x1, other arithmetic: 58.3 us -> 12.3 us
    another operation x2 -> x1, local copies, waits for them, and re-layouts: 15.3 us -> 1.32 us  [shards(): jnp.moveaxis(block_outs, 0, 1)]
    all_to_all x2 -> x0, local copies, waits for them, and re-layouts: 8.74 us -> none  [shards(): lax.all_to_all(all_rows, 'mp', split_axis=1, concat_axis=2, tiled=True)]
    unnamed x20 -> x30, local copies, waits for them, and re-layouts: 16.7 us -> 15.6 us
where the time goes in v1:
time: 308 us; the launch traced here: 307 us
  local copies, waits for them, and re-layouts  86.5 us (28%)
  matrix products  82.8 us (27%)
  waiting for transfers between devices  57.3 us (19%)
  other arithmetic  29.6 us (10%)
  blocking collectives  27.4 us (9%)
  loops' own time  11.5 us (4%)
  starting transfers between devices  11.4 us (4%)
    all_to_all x1, waiting for transfers between devices, shards(): lax.all_to_all(by_head, 'mp', split_axis=3, concat_axis=1, tiled=True)  42.5 us
    gather x4, local copies, waits for them, and re-layouts, shards(): picked = jnp.take(processed, local_index[slot_index], axis=1)  38.6 us
    dot_general x16, matrix products, attend(): jnp.einsum('mqhe,mkhe->mhqk', queries, key_rows, preferred_element_type=j...  38 us
    all_to_all x1, blocking collectives, shards(): lax.all_to_all(decoded, 'ens', split_axis=2, concat_axis=0, tiled=True)  27.4 us
    dot_general x16, matrix products, attend(): jnp.einsum('mhqk,mkhe->mqhe', weights, value_rows, preferred_element_type...  23.2 us
    unnamed x30, local copies, waits for them, and re-layouts  15.6 us
    all_to_all x1, waiting for transfers between devices, shards(): incoming = lax.all_to_all(jnp.stack(shards_2), 'mp', 0, 0)  14.8 us
    unnamed x1, other arithmetic  12.3 us
  transfers between devices with their start and end apart: 2, of which 2 were waited for; matrix products, arithmetic and copies ran while one was open for 0% of the time, Pallas kernels for 0%

profile of v1, /device:TPU:8, one launch (start us, length us, event | category | flops | bytes accessed | tf_op | source)
XLA Modules:
  0.0 306.5 jit_solution(17100917207828871414)
XLA Ops:
  3.2 8.3 %convolution_convert_fusion = bf16[512,3072]{1,0:T(8,128)(2,1)} fusion(bf16[1024,3072]{1,0:T(8,128)(2,1)} %param.14, bf16[1,512,1024]{2,1,0:T(8,128)(2,1)} %param.12, f32[1024]{0:T(1024)} %param.13, f32[512]{0:T(512)S(1)} %add_rsqrt_fusion, f32[512]{0:T(512)S(1)} %broadcast_multiply_fusion), kind=kOutput, calls=%fused_computation.28 | convolution fusion | flops 3225419776 | bytes 10493952 | tf_op jit(solution)/shard_map/mtd,de->mte/dot_general | solution.py:49
  11.5 4.7 %copy.52 = bf16[512,3072]{0,1:T(8,128)(2,1)} copy(bf16[512,3072]{1,0:T(8,128)(2,1)} %convolution_convert_fusion) | data formatting | bytes 6291456 | tf_op jit(solution)/shard_map/convert_element_type | solution.py:49
  16.2 3.9 %copy.53 = bf16[1,512,3,16,64]{1,4,2,0,3:T(8,128)(2,1)} copy(bf16[1,512,3,16,64]{1,4,3,2,0:T(8,128)(2,1)} %bitcast.195) | data formatting | bytes 6291456 | tf_op jit(solution)/shard_map/reshape | solution.py:52
  20.2 6.5 %all-to-all-start = ((bf16[1,512,3,16,64]{1,4,2,0,3:T(8,128)(2,1)}), bf16[1,512,3,16,64]{1,4,2,0,3:T(8,128)(2,1)}, u32[]{:S(2)}, u32[]{:S(2)}) async-start(bf16[1,512,3,16,64]{1,4,2,0,3:T(8,128)(2,1)} %copy.53), calls=%async_computation | async-start | bytes 6291456 | tf_op jit(solution)/shard_map/all_to_all | solution.py:53
  26.8 42.5 %all-to-all-done = bf16[1,512,3,16,64]{1,4,2,0,3:T(8,128)(2,1)} async-done(((bf16[1,512,3,16,64]{1,4,2,0,3:T(8,128)(2,1)}), bf16[1,512,3,16,64]{1,4,2,0,3:T(8,128)(2,1)}, u32[]{:S(2)}, u32[]{:S(2)}) %all-to-all-start) | async-done | bytes 3145760 | tf_op jit(solution)/shard_map/all_to_all | solution.py:53
  74.1 92.6 %while.12 = (s32[]{:T(128)}, bf16[16,1,512,1,64]{2,4,3,1,0:T(8,128)(2,1)}, s32[16]{0:T(128)S(1)}, bf16[1,9216,1,64]{1,3,2,0:T(8,128)(2,1)S(1)}, bf16[1,8192,1,64...) while((s32[]{:T(128)}, ...), condition=%wide.region_5.6_spmd, body=%wide.region_2.5_spmd.sunk | while | flops 210803712 | bytes 9991916 | solution.py:66
  87.1 2.4 fusion.70
  98.6 2.4 fusion.70
  104.4 2.4 fusion.70
  116.0 2.4 fusion.70
  127.6 2.4 fusion.70
  150.7 2.4 fusion.70
  178.0 4.9 %all-to-all-start.1 = ((bf16[16,1,512,1,64]{2,4,3,1,0:T(8,128)(2,1)}), bf16[16,1,512,1,64]{2,4,3,1,0:T(8,128)(2,1)S(1)}, u32[]{:S(2)}, u32[]{:S(2)}) async-start(bf16[16,1,512,1,64]{2,4,3,1,0:T(8,128)(2,1)} %fusion.37), calls=%async_computation.1 | async-start | bytes 2097152 | tf_op jit(solution)/shard_map/all_to_all | solution.py:71
  183.0 14.8 %all-to-all-done.1 = bf16[16,1,512,1,64]{2,4,3,1,0:T(8,128)(2,1)S(1)} async-done(((bf16[16,1,512,1,64]{2,4,3,1,0:T(8,128)(2,1)}), bf16[16,1,512,1,64]{2,4,3,1,0:T(8,128)(2,1)S(1)}, u32[]{:S(2)}, u32[]{:S(2)}) %all-to-all-start.1) | async-done | bytes 1048608 | tf_op jit(solution)/shard_map/all_to_all | solution.py:71
  198.7 2.8 fusion.31
  201.5 9.6 %gather_fusion = bf16[2048,1024]{1,0:T(8,128)(2,1)} fusion(bf16[512,1024]{1,0:T(8,128)(2,1)S(1)} %fusion.31, s32[2048]{0:T(1024)S(1)} %get-tuple-element.115), kind=kCustom, calls=%fused_computation.clone | custom fusion | bytes 8396800 | tf_op jit(solution)/shard_map/jit(_take)/gather | solution.py:79
  211.2 9.7 %gather_fusion.1 = bf16[2048,1024]{1,0:T(8,128)(2,1)} fusion(bf16[512,1024]{1,0:T(8,128)(2,1)S(1)} %fusion.31, s32[2048]{0:T(1024)S(1)} %get-tuple-element.116), kind=kCustom, calls=%fused_computation.1.clone | custom fusion | bytes 8396800 | tf_op jit(solution)/shard_map/jit(_take)/gather | solution.py:79
  220.9 9.7 %gather_fusion.2 = bf16[2048,1024]{1,0:T(8,128)(2,1)} fusion(bf16[512,1024]{1,0:T(8,128)(2,1)S(1)} %fusion.31, s32[2048]{0:T(1024)S(1)} %get-tuple-element.117), kind=kCustom, calls=%fused_computation.2.clone | custom fusion | bytes 8396800 | tf_op jit(solution)/shard_map/jit(_take)/gather | solution.py:79
  230.5 9.7 %gather_fusion.3 = bf16[2048,1024]{1,0:T(8,128)(2,1)} fusion(bf16[512,1024]{1,0:T(8,128)(2,1)S(1)} %fusion.31, s32[2048]{0:T(1024)S(1)} %get-tuple-element.118), kind=kCustom, calls=%fused_computation.3.clone | custom fusion | bytes 8396800 | tf_op jit(solution)/shard_map/jit(_take)/gather | solution.py:79
  240.2 10.4 %fusion.23 = bf16[1,100,2048]{2,1,0:T(8,128)(2,1)} fusion(bf16[100,1024]{1,0:T(8,128)(2,1)S(1)} %copy-done.5, bf16[2048,1024]{1,0:T(8,128)(2,1)} %gather_fusion.3, bf16[2048,1024]{1,0:T(8,128)(2,1)} %gather_fusion.2, bf16[2048,1024]{1,0:T(8,128)(2,1)} %gather_fusion.1, bf16[2048,1024]{1,0:T(8,128)(2,1)} %gather_fusion, f32[2048]{0:T(1024)S(1)} %bitcast.225, ...), kind=kOutput, calls=%fused_computation.41 | convolution fusion | flops 453189632 | bytes 17432576 | tf_op jit(solution)/shard_map/vd,mgd->mvg/dot_general | solution.py:81
  253.5 12.3 %reduce.12 = bf16[2048,100]{1,0:T(8,128)(2,1)} reduce(bf16[2048,1,100]{2,1,0:T(2,128)(2,1)S(1)} %bitcast.213, bf16[]{:T(256)} %broadcast.155), dimensions={1}, to_apply=%bitcast.171.reduce_sub_computation | reduce | bytes 819202
  265.8 2.6 reshape.228
  268.3 27.4 %all_to_all.32 = bf16[16,2,6400]{2,1,0:T(2,128)(2,1)S(1)} all-to-all(bf16[16,2,6400]{2,1,0:T(2,128)(2,1)S(1)} %reshape.228), channel_id=1, replica_groups=mesh['ens'=16,'mp'=16] {'ens'}, dimensions={0} | all-to-all | bytes 819200 | tf_op jit(solution)/shard_map/all_to_all | solution.py:84
  298.0 3.8 %copy.57 = bf16[1,100,2048]{2,0,1:T(2,128)(2,1)} copy(bf16[1,100,2048]{1,0,2:T(2,128)(2,1)S(1)} %bitcast.212) | data formatting | bytes 819200 | tf_op jit(solution)/shard_map/all_to_all | solution.py:84
  (160 shorter events, 97.0 us)
Async XLA Ops:
  0.0 198.7 %copy-start = (bf16[1024,1024]{1,0:T(8,128)(2,1)S(1)}, bf16[1024,1024]{1,0:T(8,128)(2,1)}, u32[]{:S(2)}) copy-start(bf16[1024,1024]{1,0:T(8,128)(2,1)} %param.15) | copy-start | bytes 6291460
  20.2 6.5 %copy-start.3 = (s32[4,2048]{1,0:T(4,128)S(1)}, s32[4,2048]{1,0:T(4,128)}, u32[]{:S(2)}) copy-start(s32[4,2048]{1,0:T(4,128)} %param.16) | copy-start | bytes 98308
  20.2 49.1 %all-to-all-start = ((bf16[1,512,3,16,64]{1,4,2,0,3:T(8,128)(2,1)}), bf16[1,512,3,16,64]{1,4,2,0,3:T(8,128)(2,1)}, u32[]{:S(2)}, u32[]{:S(2)}) async-start(bf16[1,512,3,16,64]{1,4,2,0,3:T(8,128)(2,1)} %copy.53), calls=%async_computation | async-start | bytes 6291456 | tf_op jit(solution)/shard_map/all_to_all | solution.py:53
  166.7 16.2 %copy-start.4 = (f32[4,2048]{1,0:T(4,128)S(1)}, f32[4,2048]{1,0:T(4,128)}, u32[]{:S(2)}) copy-start(f32[4,2048]{1,0:T(4,128)} %param.17) | copy-start | bytes 98308
  178.0 19.7 %all-to-all-start.1 = ((bf16[16,1,512,1,64]{2,4,3,1,0:T(8,128)(2,1)}), bf16[16,1,512,1,64]{2,4,3,1,0:T(8,128)(2,1)S(1)}, u32[]{:S(2)}, u32[]{:S(2)}) async-start(bf16[16,1,512,1,64]{2,4,3,1,0:T(8,128)(2,1)} %fusion.37), calls=%async_computation.1 | async-start | bytes 2097152 | tf_op jit(solution)/shard_map/all_to_all | solution.py:71
  197.7 1.0 copy-start.1
  230.5 9.7 %copy-start.5 = (bf16[100,1024]{1,0:T(8,128)(2,1)S(1)}, bf16[100,1024]{1,0:T(8,128)(2,1)}, u32[]{:S(2)}) copy-start(bf16[100,1024]{1,0:T(8,128)(2,1)} %param.18) | copy-start | bytes 614404
  298.0 7.7 %copy-start.2 = (f32[100,128]{1,0:T(8,128)S(1)}, f32[100,128]{1,0:T(8,128)}, u32[]{:S(2)}) copy-start(f32[100,128]{1,0:T(8,128)} %param.19) | copy-start | bytes 153604
